TPU v7x, 32 devices: a whole 2x2x4 slice. The times are simulated.
32 devices in a mesh: row: 4 (over y, x), col: 8 (over z, core).
Axes of the slice: x: 2, y: 2, z: 4, core: 2. Of those that a mesh axis runs over, the one named last changes fastest.
Arguments:
- coupling: float32 [4, 4608, 18432], P(None, 'col', 'row'), may hold values from -0.046875 to 0.046875
- energies: float32 [18432], P(('row', 'col')), may hold values from 0.7 to 14.2
- block: float32 [18432, 16], P(('row', 'col')), may hold values from -6 to 6
Outputs:
- basis: float32 [18432, 16], P(('row', 'col'))
- projections: float32 [2, 16, 16], replicated
- factors: float32 [2, 16, 16], replicated
All inputs are finite; a program needn't handle non-finite values.
Results may differ from a plain program's by a relative error of at most 0.0003.
Values sent between devices are 32-bit elements; how exact they have to be, the bound alone decides.
No kernel may reach another device: no remote copies, remote signals or barrier semaphores. Data moves between devices by JAX's collectives and lax.ppermute only.
A program may use at most 128 MiB of HBM per device.

v0:
```python
import jax
import jax.numpy as jnp
from jax import lax
from jax.sharding import PartitionSpec as P

N = 18432
ITERS = 2
precise = lax.Precision.HIGHEST


def combined(moments_local):
    return lax.psum(moments_local, "row")


def on_device(coupling, energies, block):
    segment = block.shape[0]
    width = block.shape[1]
    column = lax.axis_index("col")
    current, energy_rows = (
        lax.all_gather(block, "col", axis=0, tiled=True),
        lax.all_gather(energies, "col", axis=0, tiled=True),
    )
    prior = jnp.zeros_like(current)
    projection_list = []
    factor_list = []
    for section in range(ITERS):
        own_rows = lax.dynamic_slice_in_dim(current, column * segment, segment, 0)
        column_block = current
        spread = lax.all_gather(own_rows, "row", axis=0, tiled=True)
        spread = spread.reshape(coupling.shape[0], segment, width)
        direct = lax.psum_scatter(
            jnp.einsum("aig,gk->aik", coupling, column_block, precision=precise),
            "row",
            scatter_dimension=0,
            tiled=True,
        ).reshape(segment, width)
        partial_value = jnp.einsum("aig,aik->gk", coupling, spread, precision=precise)
        transposed = lax.psum(partial_value, "col")
        direct_rows = lax.all_gather(direct, "col", axis=0, tiled=True)
        product = energy_rows[:, None] * current + direct_rows + transposed
        stacked = jnp.concatenate([current, prior, product], axis=1)
        moments = combined(jnp.einsum("nk,nl->kl", stacked, stacked, precision=precise)) / N
        projection = moments[:width, 2 * width :]
        cross = moments[width : 2 * width, 2 * width :]
        weights = jnp.concatenate([-projection, -cross, jnp.eye(width, dtype=jnp.float32)], axis=0)
        gram_matrix = jnp.dot(
            weights.T, jnp.dot(moments, weights, precision=precise), precision=precise
        )
        factor = jnp.linalg.cholesky(gram_matrix)
        residual = (
            product
            - jnp.dot(current, projection, precision=precise)
            - jnp.dot(prior, cross, precision=precise)
        )
        prior = current
        current = jax.scipy.linalg.solve_triangular(factor, residual.T, lower=True).T
        projection_list.append(projection)
        factor_list.append(factor)
    basis = lax.dynamic_slice_in_dim(current, column * segment, segment, 0)
    return (basis, jnp.stack(projection_list), jnp.stack(factor_list))


def solution(mesh):
    placed = (P(None, "col", "row"), P(("row", "col")), P(("row", "col"), None))
    return jax.shard_map(
        on_device,
        mesh=mesh,
        in_specs=placed,
        out_specs=(P(("row", "col"), None), P(), P()),
        check_vma=False,
    )
```

profile of v0, /device:TPU:0, one launch (start us, length us, event | category | flops | bytes accessed | tf_op | source)
XLA Modules:
  0.0 340.6 jit_solution(8555709565530399333)
XLA Ops:
  8.0 16.3 %all-gather.2 = f32[8,576,16]{1,2,0:T(8,128)S(1)} all-gather(f32[1,576,16]{1,2,0:T(8,128)} %bitcast.93), channel_id=1, replica_groups=mesh['row'=4,'col'=8] {'col'}, dimensions={0}, use_global_device_ids=true | all-gather | bytes 331776 | tf_op jit(solution)/shard_map/all_gather | solution.py:20
  24.6 40.0 %fusion.44 = f32[4,576,16]{1,2,0:T(8,128)} fusion(f32[4,576,4608]{2,1,0:T(8,128)} %param.6, f32[4608,16,1]{0,1,2:T(8,128)S(1)} %reshape.46), kind=kOutput, calls=%fused_computation.77 | convolution fusion | flops 2038431744 | bytes 42909696 | tf_op jit(solution)/shard_map/aig,gk->aik/dot_general | solution.py:32
  64.9 8.8 %all-gather.3 = f32[4,576,16]{1,2,0:T(8,128)S(1)} all-gather(f32[1,576,16]{1,2,0:T(8,128)S(1)} %dynamic-slice_bitcast_fusion.2), channel_id=1, replica_groups=mesh['row'=4,'col'=8] {'row'}, dimensions={0}, use_global_device_ids=true | all-gather | bytes 184320 | tf_op jit(solution)/shard_map/all_gather | solution.py:29
  73.6 24.6 %convolution_bitcast_fusion.3 = f32[4608,16]{0,1:T(8,128)} fusion(f32[4,576,16]{1,2,0:T(8,128)S(1)} %all-gather.3, f32[4,576,4608]{2,1,0:T(8,128)} %param.6), kind=kOutput, calls=%fused_computation.9 | convolution fusion | flops 2038431744 | bytes 42909696 | tf_op jit(solution)/shard_map/aig,aik->gk/dot_general | solution.py:37
  99.9 27.3 %all-reduce = f32[4608]{0:T(1024)S(1)} all-reduce(f32[4608]{0:T(1024)S(1)} %dynamic-update-slice.2), channel_id=1, replica_groups=mesh['row'=4,'col'=8] {'col'}, use_global_device_ids=true, to_apply=%add | all-reduce | flops 4608 | bytes 36864
  127.2 0.9 copy.10
  128.2 24.6 %all-gather = f32[1,4608,16]{2,0,1:T(1,128)S(1)} all-gather(f32[1,576,16]{2,0,1:T(1,128)S(1)} %copy.10), channel_id=2, replica_groups=mesh['row'=4,'col'=8] {'col'}, dimensions={1}, use_global_device_ids=true | all-gather | bytes 331776 | tf_op jit(solution)/shard_map/all_gather | solution.py:39
  152.7 2.2 copy.11
  154.9 1.0 fusion.19
  156.0 0.9 fusion.5
  156.9 15.3 %psum.29 = f32[48,48]{1,0:T(8,128)S(1)} all-reduce(f32[48,48]{1,0:T(8,128)S(1)} %fusion.5), channel_id=1, replica_groups=mesh['row'=4,'col'=8] {'row'}, use_global_device_ids=true, to_apply=%region_2.0 | all-reduce | flops 2304 | bytes 18432 | tf_op jit(solution)/shard_map/psum | solution.py:12
  172.3 0.7 slice_bitcast_fusion.1
  173.6 1.5 cholesky.44
  175.1 0.6 compare_reduce_fusion.1
  175.7 0.6 fusion.37
  176.4 1.2 custom-call.6
  178.6 39.3 %convolution_bitcast_fusion.4 = f32[4,576,16]{1,2,0:T(8,128)} fusion(f32[4,576,4608]{2,1,0:T(8,128)} %param.6, f32[16,4608]{1,0:T(8,128)S(1)} %fusion.23), kind=kOutput, calls=%fused_computation.10 | convolution fusion | flops 2038431744 | bytes 42909696 | tf_op jit(solution)/shard_map/aig,gk->aik/dot_general | solution.py:32
  218.1 8.7 %all-gather.4 = f32[4,576,16]{1,2,0:T(8,128)S(1)} all-gather(f32[1,576,16]{1,2,0:T(8,128)S(1)} %dynamic-slice_bitcast_fusion.1), channel_id=1, replica_groups=mesh['row'=4,'col'=8] {'row'}, dimensions={0}, use_global_device_ids=true | all-gather | bytes 184320 | tf_op jit(solution)/shard_map/all_gather | solution.py:29
  226.8 24.6 %convolution_bitcast_fusion.2 = f32[4608,16]{0,1:T(8,128)} fusion(f32[4,576,16]{1,2,0:T(8,128)S(1)} %all-gather.4, f32[4,576,4608]{2,1,0:T(8,128)} %param.6), kind=kOutput, calls=%fused_computation.8 | convolution fusion | flops 2038431744 | bytes 42909696 | tf_op jit(solution)/shard_map/aig,aik->gk/dot_general | solution.py:37
  251.4 0.9 copy.15
  252.4 28.0 %all-gather.1 = f32[1,4608,16]{2,0,1:T(1,128)S(1)} all-gather(f32[1,576,16]{2,0,1:T(1,128)S(1)} %copy.15), channel_id=3, replica_groups=mesh['row'=4,'col'=8] {'col'}, dimensions={1}, use_global_device_ids=true | all-gather | bytes 331776 | tf_op jit(solution)/shard_map/all_gather | solution.py:39
  280.4 2.2 copy.16
  282.6 24.1 %all-reduce.8.cloned.1.call-done = f32[4608,16]{0,1:T(8,128)} async-done(((f32[4608,16]{0,1:T(8,128)}), f32[4608,16]{0,1:T(8,128)}) %all-reduce.8.cloned.1.call-update) | async-done | bytes 294928 | tf_op jit(solution)/shard_map/psum | solution.py:38
  306.7 1.1 fusion.17
  307.7 0.8 fusion.10
  308.6 16.3 %psum.31 = f32[48,48]{1,0:T(8,128)S(1)} all-reduce(f32[48,48]{1,0:T(8,128)S(1)} %fusion.10), channel_id=1, replica_groups=mesh['row'=4,'col'=8] {'row'}, use_global_device_ids=true, to_apply=%region_8.11 | all-reduce | flops 2304 | bytes 18432 | tf_op jit(solution)/shard_map/psum | solution.py:12
  326.1 1.5 cholesky.55
  327.6 0.6 compare_reduce_fusion
  328.3 0.6 fusion.36
  328.9 1.2 custom-call.7
  331.1 0.7 dynamic-slice_bitcast_fusion
  331.8 1.3 pad_maximum_fusion
  (50 shorter events, 5.6 us)
Async XLA Ops:
  8.0 119.2 %reduce-scatter.7.cloned.1.call-start = ((), (), s32[]{:S(2)}) async-start(), calls=%async_computation.4 | async-start | bytes 204800
  24.5 73.8 %copy-start.2 = (u32[32]{0:T(128)S(1)}, u32[32]{0:T(128)}, u32[]{:S(2)}) copy-start(u32[32]{0:T(128)} %constant.50) | copy-start | bytes 388
  24.5 75.1 %copy-start.1 = (f32[576]{0:T(1024)S(1)}, f32[576]{0:T(1024)}, u32[]{:S(2)}) copy-start(f32[576]{0:T(1024)} %param.7) | copy-start | bytes 6916
  64.6 90.3 %all-reduce.6.cloned.1.call-start = ((), (), s32[]{:S(2)}) async-start(), calls=%async_computation.2 | async-start | bytes 589824 | tf_op jit(solution)/shard_map/psum | solution.py:38
  98.3 153.2 %reduce-scatter.9.cloned.1.call-start = ((), (), s32[]{:S(2)}) async-start(), calls=%async_computation.5 | async-start | bytes 204800
  127.2 124.2 %copy-start = (f32[4608]{0:T(1024)}, f32[4608]{0:T(1024)S(1)}, u32[]{:S(2)}) copy-start(f32[4608]{0:T(1024)S(1)} %all-reduce) | copy-start | bytes 55300
  218.0 88.7 %all-reduce.8.cloned.1.call-start = ((), (), s32[]{:S(2)}) async-start(), calls=%async_computation.3 | async-start | bytes 589824 | tf_op jit(solution)/shard_map/psum | solution.py:38
Sparse Core Ops, SparseCore 0:
  64.7 25.2 reduce-scatter.6
  218.1 24.4 reduce-scatter.8
Sparse Core Ops, SparseCore 1:
  98.3 55.3 all-reduce.5
  251.5 55.1 all-reduce.7
where the time goes:
time: 341 us
  blocking collectives  145 us (43%)
  matrix products  134 us (39%)
  waiting for transfers between devices  24.2 us (7%)
  between operations  16.4 us (5%)
  other arithmetic  12.2 us (4%)
  local copies, waits for them, and re-layouts  8.71 us (3%)
    dot_general x2, matrix products, on_device(): jnp.einsum('aig,gk->aik', coupling, column_block, precision=precise)  79.3 us
    all_gather x2, blocking collectives, on_device(): direct_rows = lax.all_gather(direct, 'col', axis=0, tiled=True)  52.6 us
    dot_general x2, matrix products, on_device(): jnp.einsum('aig,aik->gk', coupling, spread, precision=precise)  49.2 us
    psum x2, blocking collectives, combined(): return lax.psum(moments_local, 'row')  31.6 us
    unnamed x1, blocking collectives  27.3 us
    psum x2, waiting for transfers between devices, on_device(): transposed = lax.psum(partial_value, 'col')  24.1 us
    all_gather x2, blocking collectives, on_device(): spread = lax.all_gather(own_rows, 'row', axis=0, tiled=True)  17.5 us
    all_gather x1, blocking collectives, on_device(): lax.all_gather(block, 'col', axis=0, tiled=True)  16.3 us
  transfers between devices with their start and end apart: 4, of which 1 were waited for; matrix products, arithmetic and copies ran while one was open for 17% of the time, Pallas kernels for 0%

commit v1 on v0

--- a/solution.py
+++ b/solution.py
@@ -6,6 +6,28 @@
 N = 18432
 ITERS = 2
 precise = lax.Precision.HIGHEST
+
+
+def joined_along(blocks, dim):
+    blocks = jnp.moveaxis(blocks, 0, dim)
+    dims = blocks.shape
+    return blocks.reshape(*dims[:dim], dims[dim] * dims[dim + 1], *dims[dim + 2 :])
+
+
+def collected_by_bits(shard, axis):
+    count = lax.axis_size(axis)
+    parts = shard[None]
+    for level in range(count.bit_length() - 1):
+        bit = 1 << level
+        other = lax.ppermute(parts, axis, [(i, i ^ bit) for i in range(count)])
+        both = jnp.stack([parts, other])
+        upper = lax.axis_index(axis) >> level & 1
+        parts = jnp.where(upper == 0, both, both[::-1]).reshape(-1, *shard.shape)
+    return parts
+
+
+def gather_by_bits(shard, axis, dim):
+    return joined_along(collected_by_bits(shard, axis), dim)
 
 
 def combined(moments_local):
@@ -36,7 +58,7 @@
         ).reshape(segment, width)
         partial_value = jnp.einsum("aig,aik->gk", coupling, spread, precision=precise)
         transposed = lax.psum(partial_value, "col")
-        direct_rows = lax.all_gather(direct, "col", axis=0, tiled=True)
+        direct_rows = gather_by_bits(direct, "col", 0)
         product = energy_rows[:, None] * current + direct_rows + transposed
         stacked = jnp.concatenate([current, prior, product], axis=1)
         moments = combined(jnp.einsum("nk,nl->kl", stacked, stacked, precision=precise)) / N

time: 341 us -> 391 us (1.15)
  waiting for transfers between devices: 24.2 us -> 124 us
  blocking collectives: 145 us -> 92.3 us
  starting transfers between devices: 0.17 us -> 8.23 us
  local copies, waits for them, and re-layouts: 8.71 us -> 3.26 us
    all_gather x2 -> x0, blocking collectives: 52.6 us -> none  [on_device(): direct_rows = lax.all_gather(direct, 'col', axis=0, tiled=True)]
    unnamed x6, waiting for transfers between devices: 0.09 us -> 49.4 us
    psum x2, waiting for transfers between devices: 24.1 us -> 72.2 us  [on_device(): transposed = lax.psum(partial_value, 'col')]
    ppermute x0 -> x6, starting transfers between devices: none -> 8.06 us  [collected_by_bits(): other = lax.ppermute(parts, axis, [(i, i ^ bit) for i in range(count)])]
    all_gather x2 -> x0, local copies, waits for them, and re-layouts: 4.31 us -> none  [on_device(): direct_rows = lax.all_gather(direct, 'col', axis=0, tiled=True)]
  transfers between devices with their start and end apart: 4 -> 10, of which waited for: 1 -> 6; matrix products, arithmetic and copies ran while one was open for 17% -> 13% of each run, Pallas kernels for 0% -> 0%
where the time goes in v1:
time: 391 us
  matrix products  133 us (34%)
  waiting for transfers between devices  124 us (32%)
  blocking collectives  92.3 us (24%)
  between operations  16.5 us (4%)
  other arithmetic  12.8 us (3%)
  starting transfers between devices  8.23 us (2%)
    dot_general x2, matrix products, on_device(): jnp.einsum('aig,gk->aik', coupling, column_block, precision=precise)  79.3 us
    psum x2, waiting for transfers between devices, on_device(): transposed = lax.psum(partial_value, 'col')  72.2 us
    unnamed x6, waiting for transfers between devices  49.4 us
    dot_general x2, matrix products, on_device(): jnp.einsum('aig,aik->gk', coupling, spread, precision=precise)  49 us
    psum x2, blocking collectives, combined(): return lax.psum(moments_local, 'row')  32.5 us
    unnamed x1, blocking collectives  26 us
    all_gather x2, blocking collectives, on_device(): spread = lax.all_gather(own_rows, 'row', axis=0, tiled=True)  17.5 us
    all_gather x1, blocking collectives, on_device(): lax.all_gather(block, 'col', axis=0, tiled=True)  16.3 us
  transfers between devices with their start and end apart: 10, of which 6 were waited for; matrix products, arithmetic and copies ran while one was open for 13% of the time, Pallas kernels for 0%

profile of v1, /device:TPU:0, one launch (start us, length us, event | category | flops | bytes accessed | tf_op | source)
XLA Modules:
  0.0 390.9 jit_solution(5968175040865043137)
XLA Ops:
  8.0 16.3 %all-gather = f32[8,576,16]{1,2,0:T(8,128)S(1)} all-gather(f32[1,576,16]{1,2,0:T(8,128)} %bitcast.127), channel_id=1, replica_groups=mesh['row'=4,'col'=8] {'col'}, dimensions={0}, use_global_device_ids=true | all-gather | bytes 331776 | tf_op jit(solution)/shard_map/all_gather | solution.py:42
  24.6 40.0 %fusion.46 = f32[4,576,16]{1,2,0:T(8,128)} fusion(f32[4,576,4608]{2,1,0:T(8,128)} %param.6, f32[4608,16,1]{0,1,2:T(8,128)S(1)} %reshape.52), kind=kOutput, calls=%fused_computation.91 | convolution fusion | flops 2038431744 | bytes 42909696 | tf_op jit(solution)/shard_map/aig,gk->aik/dot_general | solution.py:54
  64.7 25.4 %reduce-scatter.7.cloned.1.call-done = f32[1,576,16]{1,2,0:T(8,128)} async-done(((f32[4,576,16]{1,2,0:T(8,128)}), f32[1,576,16]{1,2,0:T(8,128)}) %reduce-scatter.7.cloned.1.call-update) | async-done | bytes 36880
  90.2 1.3 collective-permute-done
  91.5 0.8 pad_maximum_fusion.4
  92.3 1.6 collective-permute-start.1
  93.9 8.7 %all-gather.1 = f32[4,576,16]{1,2,0:T(8,128)S(1)} all-gather(f32[1,576,16]{1,2,0:T(8,128)S(1)} %dynamic-slice_bitcast_fusion.2), channel_id=1, replica_groups=mesh['row'=4,'col'=8] {'row'}, dimensions={0}, use_global_device_ids=true | all-gather | bytes 184320 | tf_op jit(solution)/shard_map/all_gather | solution.py:51
  102.8 2.5 collective-permute-start.2
  105.2 24.5 %convolution_bitcast_fusion.3 = f32[4608,16]{0,1:T(8,128)} fusion(f32[4,576,16]{1,2,0:T(8,128)S(1)} %all-gather.1, f32[4,576,4608]{2,1,0:T(8,128)} %param.6), kind=kOutput, calls=%fused_computation.9 | convolution fusion | flops 2038431744 | bytes 42909696 | tf_op jit(solution)/shard_map/aig,aik->gk/dot_general | solution.py:59
  131.4 26.0 %all-reduce = f32[4608]{0:T(1024)S(1)} all-reduce(f32[4608]{0:T(1024)S(1)} %dynamic-update-slice.2), channel_id=1, replica_groups=mesh['row'=4,'col'=8] {'col'}, use_global_device_ids=true, to_apply=%add | all-reduce | flops 4608 | bytes 36864
  157.9 22.4 %all-reduce.6.cloned.1.call-done = f32[4608,16]{0,1:T(8,128)} async-done(((f32[4608,16]{0,1:T(8,128)}), f32[4608,16]{0,1:T(8,128)}) %all-reduce.6.cloned.1.call-update) | async-done | bytes 294928 | tf_op jit(solution)/shard_map/psum | solution.py:60
  180.3 1.0 add_add_fusion.1
  181.3 0.9 fusion.5
  182.3 16.3 %psum.29 = f32[48,48]{1,0:T(8,128)S(1)} all-reduce(f32[48,48]{1,0:T(8,128)S(1)} %fusion.5), channel_id=1, replica_groups=mesh['row'=4,'col'=8] {'row'}, use_global_device_ids=true, to_apply=%region_2.3 | all-reduce | flops 2304 | bytes 18432 | tf_op jit(solution)/shard_map/psum | solution.py:34
  199.3 1.5 cholesky.44
  201.4 0.6 fusion.39
  202.1 1.2 custom-call.6
  204.3 39.3 %convolution_bitcast_fusion.4 = f32[4,576,16]{1,2,0:T(8,128)} fusion(f32[4,576,4608]{2,1,0:T(8,128)} %param.6, f32[16,4608]{1,0:T(8,128)S(1)} %fusion.25), kind=kOutput, calls=%fused_computation.10 | convolution fusion | flops 2038431744 | bytes 42909696 | tf_op jit(solution)/shard_map/aig,gk->aik/dot_general | solution.py:54
  243.7 23.9 %reduce-scatter.9.cloned.1.call-done = f32[1,576,16]{1,2,0:T(8,128)} async-done(((f32[4,576,16]{1,2,0:T(8,128)}), f32[1,576,16]{1,2,0:T(8,128)}) %reduce-scatter.9.cloned.1.call-update) | async-done | bytes 36880
  267.6 1.4 collective-permute-done.3
  269.1 0.8 pad_maximum_fusion.5
  269.9 1.5 collective-permute-start.4
  271.5 8.8 %all-gather.2 = f32[4,576,16]{1,2,0:T(8,128)S(1)} all-gather(f32[1,576,16]{1,2,0:T(8,128)S(1)} %dynamic-slice_bitcast_fusion.1), channel_id=1, replica_groups=mesh['row'=4,'col'=8] {'row'}, dimensions={0}, use_global_device_ids=true | all-gather | bytes 184320 | tf_op jit(solution)/shard_map/all_gather | solution.py:51
  280.4 2.5 collective-permute-start.5
  282.9 24.5 %convolution_bitcast_fusion.2 = f32[4608,16]{0,1:T(8,128)} fusion(f32[4,576,16]{1,2,0:T(8,128)S(1)} %all-gather.2, f32[4,576,4608]{2,1,0:T(8,128)} %param.6), kind=kOutput, calls=%fused_computation.8 | convolution fusion | flops 2038431744 | bytes 42909696 | tf_op jit(solution)/shard_map/aig,aik->gk/dot_general | solution.py:59
  307.9 49.9 %all-reduce.8.cloned.1.call-done = f32[4608,16]{0,1:T(8,128)} async-done(((f32[4608,16]{0,1:T(8,128)}), f32[4608,16]{0,1:T(8,128)}) %all-reduce.8.cloned.1.call-update) | async-done | bytes 294928 | tf_op jit(solution)/shard_map/psum | solution.py:60
  357.8 1.0 add_add_fusion
  358.8 0.8 fusion.10
  359.6 16.3 %psum.31 = f32[48,48]{1,0:T(8,128)S(1)} all-reduce(f32[48,48]{1,0:T(8,128)S(1)} %fusion.10), channel_id=1, replica_groups=mesh['row'=4,'col'=8] {'row'}, use_global_device_ids=true, to_apply=%region_8.11 | all-reduce | flops 2304 | bytes 18432 | tf_op jit(solution)/shard_map/psum | solution.py:34
  377.2 1.5 cholesky.55
  380.0 1.2 custom-call.7
  382.2 0.7 dynamic-slice_bitcast_fusion
  (72 shorter events, 9.3 us)
Async XLA Ops:
  8.0 82.1 %reduce-scatter.7.cloned.1.call-start = ((), (), s32[]{:S(2)}) async-start(), calls=%async_computation.4 | async-start | bytes 204800
  24.5 105.3 %copy-start.1 = (u32[32]{0:T(128)S(1)}, u32[32]{0:T(128)}, u32[]{:S(2)}) copy-start(u32[32]{0:T(128)} %constant.54) | copy-start | bytes 388
  24.5 106.6 %copy-start = (f32[576]{0:T(1024)S(1)}, f32[576]{0:T(1024)}, u32[]{:S(2)}) copy-start(f32[576]{0:T(1024)} %param.7) | copy-start | bytes 6916
  64.6 115.7 %all-reduce.6.cloned.1.call-start = ((), (), s32[]{:S(2)}) async-start(), calls=%async_computation.2 | async-start | bytes 589824 | tf_op jit(solution)/shard_map/psum | solution.py:60
  90.1 1.4 collective-permute-start
  92.3 10.4 %collective-permute-start.1 = (f32[2,576,16]{1,2,0:T(8,128)S(1)}, f32[2,576,16]{1,2,0:T(8,128)S(1)}, u32[]{:S(2)}, u32[]{:S(2)}) collective-permute-start(f32[2,576,16]{1,2,0:T(8,128)S(1)} %get-tuple-element.8), channel_id=1, source_target_pairs={{0,2},{1,3},{2,0},{3,1},{4,6},{5,7},{6,4},{7,5},{8,10},{9,11},{10,... | collective-permute-start | bytes 221192 | tf_op jit(solution)/shard_map/ppermute | solution.py:22
  102.8 54.8 %collective-permute-start.2 = (f32[4,576,16]{1,0,2:T(4,128)S(1)}, f32[4,576,16]{1,0,2:T(4,128)S(1)}, u32[]{:S(2)}, u32[]{:S(2)}) collective-permute-start(f32[4,576,16]{1,0,2:T(4,128)S(1)} %copy.17), channel_id=1, source_target_pairs={{0,4},{1,5},{2,6},{3,7},{4,0},{5,1},{6,2},{7,3},{8,12},{9,13},{10,... | collective-permute-start | bytes 442376 | tf_op jit(solution)/shard_map/ppermute | solution.py:22
  129.8 137.9 %reduce-scatter.9.cloned.1.call-start = ((), (), s32[]{:S(2)}) async-start(), calls=%async_computation.5 | async-start | bytes 204800
  243.6 114.1 %all-reduce.8.cloned.1.call-start = ((), (), s32[]{:S(2)}) async-start(), calls=%async_computation.3 | async-start | bytes 589824 | tf_op jit(solution)/shard_map/psum | solution.py:60
  267.6 1.4 collective-permute-start.3
  269.9 10.4 %collective-permute-start.4 = (f32[2,576,16]{1,2,0:T(8,128)S(1)}, f32[2,576,16]{1,2,0:T(8,128)S(1)}, u32[]{:S(2)}, u32[]{:S(2)}) collective-permute-start(f32[2,576,16]{1,2,0:T(8,128)S(1)} %get-tuple-element.6), channel_id=1, source_target_pairs={{0,2},{1,3},{2,0},{3,1},{4,6},{5,7},{6,4},{7,5},{8,10},{9,11},{10,... | collective-permute-start | bytes 221192 | tf_op jit(solution)/shard_map/ppermute | solution.py:22
  280.4 27.1 %collective-permute-start.5 = (f32[4,576,16]{1,0,2:T(4,128)S(1)}, f32[4,576,16]{1,0,2:T(4,128)S(1)}, u32[]{:S(2)}, u32[]{:S(2)}) collective-permute-start(f32[4,576,16]{1,0,2:T(4,128)S(1)} %copy.22), channel_id=1, source_target_pairs={{0,4},{1,5},{2,6},{3,7},{4,0},{5,1},{6,2},{7,3},{8,12},{9,13},{10,... | collective-permute-start | bytes 442376 | tf_op jit(solution)/shard_map/ppermute | solution.py:22
Sparse Core Ops, SparseCore 0:
  64.7 25.2 reduce-scatter.6
  243.8 23.8 reduce-scatter.8
Sparse Core Ops, SparseCore 1:
  129.9 50.4 all-reduce.5
  307.5 50.2 all-reduce.7
